TPU v7x, 32 devices: a whole 2x2x4 slice. The times are simulated.
32 devices in a mesh: seq: 4 (over z), tensor: 2 (over y), section: 4 (over x, core).
Axes of the slice: x: 2, y: 2, z: 4, core: 2. Of those that a mesh axis runs over, the one named last changes fastest.
Arguments:
- dec_inputs: bfloat16 [4, 1024, 4096], P('section', 'seq'), may hold values from -64 to 64
- w_query: bfloat16 [4, 4096, 512], P('section', None, 'tensor')
- w_key: bfloat16 [4, 4096, 512], P('section', None, 'tensor')
- w_value: bfloat16 [4, 4096, 512], P('section', None, 'tensor'), may hold values from -0.09375 to 0.09375
- ctx_grad: bfloat16 [4, 1024, 512], P('section', 'seq', 'tensor'), may hold values from -96 to 96
- encoded: bfloat16 [448, 4096], P('seq'), may hold values from -11 to 11
- enc_lengths: int32 [4], replicated, may hold values from 0 to 112, as said below
Outputs:
- dec_grad: bfloat16 [4, 1024, 4096], P('section', 'seq', 'tensor')
- enc_grad: bfloat16 [448, 4096], P('seq', ('tensor', 'section'))
Inputs may be any that keep to these rules, and one draw needn't show every extreme that they name: `enc_lengths`: each block holds a prefix of valid tokens; in every draw some block is wholly valid and blocks may be empty.
All inputs are finite; a program needn't handle non-finite values.
Results may differ from a plain program's by a relative error of at most 0.018.
Values may be sent and summed in bfloat16 or wider, within the bound.
A program may use at most 64 MiB of HBM per device.

v0:
```python
import math
import jax
import jax.numpy as jnp
from jax import lax
from jax.sharding import PartitionSpec as P

masked_fill = -1e30


def body(dec_inputs, w_query, w_key, w_value, ctx_grad, encoded, enc_lengths):
    inputs = dec_inputs[0]
    wq_own = w_query[0]
    wk_own = w_key[0]
    wv_own = w_value[0]
    dout = ctx_grad[0]
    scale = 1.0 / math.sqrt(wq_own.shape[1])
    blocks = enc_lengths.shape[0]
    kdev = encoded.shape[0]
    query = jnp.dot(inputs, wq_own, preferred_element_type=jnp.float32).astype(jnp.bfloat16)
    key = jnp.dot(encoded, wk_own, preferred_element_type=jnp.float32).astype(jnp.bfloat16)
    value = jnp.dot(encoded, wv_own, preferred_element_type=jnp.float32).astype(jnp.bfloat16)
    key_all, value_all = (
        lax.all_gather(key, "seq", axis=0, tiled=True),
        lax.all_gather(value, "seq", axis=0, tiled=True),
    )
    limit = jnp.broadcast_to(enc_lengths[:, None], (blocks, kdev)).reshape(-1)
    slots = lax.broadcasted_iota(jnp.int32, (blocks, kdev), 1).reshape(-1)
    valid = (slots < limit)[None, :]
    scores = jnp.einsum("qd,kd->qk", query, key_all, preferred_element_type=jnp.float32) * scale
    scores = jnp.where(valid, scores, masked_fill)
    top = jnp.max(scores, axis=1, keepdims=True)
    expd = jnp.where(valid, jnp.exp(scores - top), 0.0)
    probs = expd / jnp.sum(expd, axis=1, keepdims=True)
    dprob = jnp.einsum("qd,kd->qk", dout, value_all, preferred_element_type=jnp.float32)
    delta = jnp.sum(probs * dprob, axis=1, keepdims=True)
    dscore = (probs * (dprob - delta) * scale).astype(jnp.bfloat16)
    probs_b = probs.astype(jnp.bfloat16)
    dquery = jnp.dot(dscore, key_all, preferred_element_type=jnp.float32).astype(jnp.bfloat16)
    dkey_part = jnp.einsum("qk,qd->kd", dscore, query, preferred_element_type=jnp.float32)
    dvalue_part = jnp.einsum("qk,qd->kd", probs_b, dout, preferred_element_type=jnp.float32)
    dkey_sum, dvalue_sum = (
        lax.psum_scatter(
            dkey_part.astype(jnp.bfloat16), "seq", scatter_dimension=0, tiled=True
        ).astype(jnp.float32),
        lax.psum_scatter(
            dvalue_part.astype(jnp.bfloat16), "seq", scatter_dimension=0, tiled=True
        ).astype(jnp.float32),
    )
    dkey = dkey_sum.astype(jnp.bfloat16)
    dvalue = dvalue_sum.astype(jnp.bfloat16)
    input_term = jnp.einsum("qd,ed->qe", dquery, wq_own, preferred_element_type=jnp.float32)
    dec_grad = lax.psum_scatter(
        input_term.astype(jnp.bfloat16), "tensor", scatter_dimension=1, tiled=True
    )
    encoder_term = jnp.einsum("kd,ed->ke", dkey, wk_own, preferred_element_type=jnp.float32)
    encoder_term = encoder_term + jnp.einsum(
        "kd,ed->ke", dvalue, wv_own, preferred_element_type=jnp.float32
    )
    enc_grad = lax.psum_scatter(
        encoder_term.astype(jnp.bfloat16), ("tensor", "section"), scatter_dimension=1, tiled=True
    )
    return (dec_grad[None, :, :], enc_grad)


def solution(mesh):
    in_specs = (
        P("section", "seq", None),
        P("section", None, "tensor"),
        P("section", None, "tensor"),
        P("section", None, "tensor"),
        P("section", "seq", "tensor"),
        P("seq", None),
        P(),
    )
    out_specs = (P("section", "seq", "tensor"), P("seq", ("tensor", "section")))
    return jax.shard_map(body, mesh=mesh, in_specs=in_specs, out_specs=out_specs, check_vma=False)
```

profile of v0, /device:TPU:0, one launch (start us, length us, event | category | flops | bytes accessed | tf_op | source)
XLA Modules:
  0.0 163.3 jit_solution(12802926421233766787)
XLA Ops:
  7.2 0.0 copy-start
  7.2 0.0 copy-start.2
  7.2 0.0 reduce-scatter.7.cloned.1.call-start
  7.2 0.9 iota_compare_fusion
  8.1 0.1 lt.11
  8.2 0.0 copy-start.1
  8.2 2.5 %fusion.18 = bf16[112,256]{1,0:T(8,128)(2,1)S(1)} fusion(bf16[112,4096]{1,0:T(8,128)(2,1)} %param.12, bf16[1,4096,256]{2,1,0:T(8,128)(2,1)} %param.9), kind=kOutput, calls=%fused_computation.21 | convolution fusion | flops 234909696 | bytes 3072000 | tf_op jit(solution)/shard_map/dot_general | solution.py:20
  10.7 0.0 copy-start.3
  10.7 15.6 %all_gather.6 = bf16[448,256]{1,0:T(8,128)(2,1)S(1)} all-gather(bf16[112,256]{1,0:T(8,128)(2,1)S(1)} %fusion.18), channel_id=1, replica_groups=mesh['seq'=4,'tensor'=2,'section'=4] {'seq'}, dimensions={0}, use_global_device_ids=true | all-gather | bytes 286720 | tf_op jit(solution)/shard_map/all_gather | solution.py:23
  26.4 0.0 copy-done.2
  26.4 0.0 copy-done.1
  26.4 0.4 fusion.21
  26.8 14.2 %all_gather.7 = bf16[448,256]{1,0:T(8,128)(2,1)S(1)} all-gather(bf16[112,256]{1,0:T(8,128)(2,1)S(1)} %fusion.21), channel_id=1, replica_groups=mesh['seq'=4,'tensor'=2,'section'=4] {'seq'}, dimensions={0}, use_global_device_ids=true | all-gather | bytes 286720 | tf_op jit(solution)/shard_map/all_gather | solution.py:24
  41.0 0.0 copy-done
  41.0 0.0 copy-done.3
  41.0 0.0 copy-start.4
  41.0 0.7 fusion.13
  41.7 0.3 fusion.30
  42.0 0.1 fusion.25
  42.2 0.0 copy-done.4
  42.2 0.3 multiply_reduce_fusion
  42.5 0.2 multiply_convert_fusion
  42.7 0.9 convolution_convert_fusion.2
  43.6 0.0 reduce-scatter.7.cloned.1.call-update
  43.6 0.0 reduce-scatter.9.cloned.1.call-start
  43.7 1.0 convolution_convert_fusion.1
  44.6 0.0 reduce-scatter.9.cloned.1.call-update
  44.6 0.0 reduce-scatter.11.cloned.1.call-start
  44.7 19.7 %reduce-scatter.7.cloned.1.call-done = bf16[112,256]{1,0:T(8,128)(2,1)} async-done(((bf16[448,256]{1,0:T(8,128)(2,1)}), bf16[112,256]{1,0:T(8,128)(2,1)}) %reduce-scatter.7.cloned.1.call-update) | async-done | bytes 57360 | tf_op jit(solution)/shard_map/reduce_scatter | solution.py:42
  64.4 3.7 %fusion.4 = f32[112,4096]{1,0:T(8,128)} fusion(bf16[112,256]{1,0:T(8,128)(2,1)} %reduce-scatter.7.cloned.1.call-done, bf16[1,4096,256]{2,1,0:T(8,128)(2,1)} %param.9), kind=kOutput, calls=%fused_computation.6 | convolution fusion | flops 234881024 | bytes 3989504 | tf_op jit(solution)/shard_map/kd,ed->ke/dot_general | solution.py:55
  68.1 16.5 %reduce-scatter.9.cloned.1.call-done = bf16[112,256]{1,0:T(8,128)(2,1)} async-done(((bf16[448,256]{1,0:T(8,128)(2,1)}), bf16[112,256]{1,0:T(8,128)(2,1)}) %reduce-scatter.9.cloned.1.call-update) | async-done | bytes 57360 | tf_op jit(solution)/shard_map/reduce_scatter | solution.py:45
  84.6 3.9 %fusion = bf16[112,4096]{1,0:T(8,128)(2,1)} fusion(f32[112,4096]{1,0:T(8,128)} %fusion.4, bf16[112,256]{1,0:T(8,128)(2,1)} %reduce-scatter.9.cloned.1.call-done, bf16[1,4096,256]{2,1,0:T(8,128)(2,1)} %param.10), kind=kOutput, calls=%fused_computation.2 | convolution fusion | flops 235798528 | bytes 4907008 | tf_op jit(solution)/shard_map/kd,ed->ke/dot_general | solution.py:56
  88.4 0.0 reduce-scatter.11.cloned.1.call-update
  88.5 0.0 reduce-scatter.5.cloned.1.call-start
  88.5 2.3 %convolution_convert_fusion = bf16[256,4096]{1,0:T(8,128)(2,1)} fusion(bf16[1,4096,256]{2,1,0:T(8,128)(2,1)S(1)} %copy-done, bf16[256,448]{0,1:T(8,128)(2,1)S(1)} %multiply_convert_fusion, bf16[448,256]{1,0:T(8,128)(2,1)S(1)} %all_gather.6), kind=kOutput, calls=%fused_computation | convolution fusion | flops 596705280 | bytes 4653056 | tf_op jit(solution)/shard_map/qd,ed->qe/dot_general | solution.py:51
  90.8 0.0 reduce-scatter.5.cloned.1.call-update
  90.9 31.5 %reduce-scatter.11.cloned.1.call-done = bf16[112,512]{1,0:T(8,128)(2,1)} async-done(((bf16[112,4096]{1,0:T(8,128)(2,1)}), bf16[112,512]{1,0:T(8,128)(2,1)}) %reduce-scatter.11.cloned.1.call-update) | async-done | bytes 114704 | tf_op jit(solution)/shard_map/reduce_scatter | solution.py:59
  122.3 34.5 %reduce-scatter.5.cloned.1.call-done = bf16[256,2048]{1,0:T(8,128)(2,1)} async-done(((bf16[256,4096]{1,0:T(8,128)(2,1)}), bf16[256,2048]{1,0:T(8,128)(2,1)}) %reduce-scatter.5.cloned.1.call-update) | async-done | bytes 1048592 | tf_op jit(solution)/shard_map/reduce_scatter | solution.py:52
Async XLA Ops:
  7.2 33.8 %copy-start = (bf16[1,4096,256]{2,1,0:T(8,128)(2,1)S(1)}, bf16[1,4096,256]{2,1,0:T(8,128)(2,1)}, u32[]{:S(2)}) copy-start(bf16[1,4096,256]{2,1,0:T(8,128)(2,1)} %param.8) | copy-start | bytes 6291460
  7.2 19.2 %copy-start.2 = (bf16[112,4096]{1,0:T(8,128)(2,1)S(1)}, bf16[112,4096]{1,0:T(8,128)(2,1)}, u32[]{:S(2)}) copy-start(bf16[112,4096]{1,0:T(8,128)(2,1)} %param.12) | copy-start | bytes 2752516
  7.2 57.2 %reduce-scatter.7.cloned.1.call-start = ((), (), s32[]{:S(2)}) async-start(), calls=%async_computation.5 | async-start | bytes 286720 | tf_op jit(solution)/shard_map/reduce_scatter | solution.py:42
  8.2 18.1 %copy-start.1 = (bf16[1,4096,256]{2,1,0:T(8,128)(2,1)S(1)}, bf16[1,4096,256]{2,1,0:T(8,128)(2,1)}, u32[]{:S(2)}) copy-start(bf16[1,4096,256]{2,1,0:T(8,128)(2,1)} %param.10) | copy-start | bytes 6291460
  10.7 30.3 %copy-start.3 = (bf16[1,256,4096]{2,1,0:T(8,128)(2,1)S(1)}, bf16[1,256,4096]{2,1,0:T(8,128)(2,1)}, u32[]{:S(2)}) copy-start(bf16[1,256,4096]{2,1,0:T(8,128)(2,1)} %param.7) | copy-start | bytes 6291460
  41.0 1.2 copy-start.4
  43.6 41.0 %reduce-scatter.9.cloned.1.call-start = ((), (), s32[]{:S(2)}) async-start(), calls=%async_computation.6 | async-start | bytes 286720 | tf_op jit(solution)/shard_map/reduce_scatter | solution.py:45
  44.6 77.7 %reduce-scatter.11.cloned.1.call-start = ((), (), s32[]{:S(2)}) async-start(), calls=%async_computation.7 | async-start | bytes 1032192 | tf_op jit(solution)/shard_map/reduce_scatter | solution.py:59
  88.5 68.4 %reduce-scatter.5.cloned.1.call-start = ((), (), s32[]{:S(2)}) async-start(), calls=%async_computation.4 | async-start | bytes 3145728 | tf_op jit(solution)/shard_map/reduce_scatter | solution.py:52
Sparse Core Ops, SparseCore 0:
  43.7 20.6 reduce-scatter.6
  66.8 17.7 reduce-scatter.8
  88.6 33.6 reduce-scatter.10
  125.0 31.7 reduce-scatter.4
where the time goes:
time: 164 us; the launch traced here: 163 us
  waiting for transfers between devices  102 us (62%)
  blocking collectives  29.8 us (18%)
  matrix products  16 us (10%)
  between operations  13.8 us (8%)
    reduce_scatter x1, waiting for transfers between devices, body(): lax.psum_scatter(input_term.astype(jnp.bfloat16), 'tensor', scatter_dimen...  34.5 us
    reduce_scatter x1, waiting for transfers between devices, body(): lax.psum_scatter(encoder_term.astype(jnp.bfloat16), ('tensor', 'section')...  31.5 us
    reduce_scatter x1, waiting for transfers between devices, body(): lax.psum_scatter(dkey_part.astype(jnp.bfloat16), 'seq', scatter_dimension...  19.7 us
    reduce_scatter x1, waiting for transfers between devices, body(): lax.psum_scatter(dvalue_part.astype(jnp.bfloat16), 'seq', scatter_dimensi...  16.5 us
    all_gather x1, blocking collectives, body(): lax.all_gather(key, 'seq', axis=0, tiled=True)  15.6 us
    all_gather x1, blocking collectives, body(): lax.all_gather(value, 'seq', axis=0, tiled=True)  14.2 us
    dot_general x1, matrix products, body(): jnp.einsum('kd,ed->ke', dvalue, wv_own, preferred_element_type=jnp.float32)  3.86 us
    dot_general x1, matrix products, body(): jnp.einsum('kd,ed->ke', dkey, wk_own, preferred_element_type=jnp.float32)  3.66 us
  transfers between devices with their start and end apart: 4, of which 4 were waited for; matrix products, arithmetic and copies ran while one was open for 4% of the time, Pallas kernels for 0%

commit v1 on v0

--- a/solution.py
+++ b/solution.py
@@ -1,3 +1,4 @@
+import functools
 import math
 import jax
 import jax.numpy as jnp
@@ -5,6 +6,24 @@
 from jax.sharding import PartitionSpec as P
 
 masked_fill = -1e30
+
+
+def bring_kinds(panel, which_dim):
+    r_now = lax.axis_size("seq")
+    w2 = lax.axis_index("seq")
+    value_now, found_now, seen_now = (r_now, w2, panel.shape[which_dim])
+    step_out, plain = (panel, 1)
+    while plain < value_now:
+        spare = lax.ppermute(
+            step_out, "seq", [(tick, (tick - plain) % value_now) for tick in range(value_now)]
+        )
+        step_out = jnp.concatenate([step_out, spare], axis=which_dim)
+        plain = 2 * plain
+    k_now = jnp.roll(step_out, found_now * seen_now, axis=which_dim)
+    return k_now
+
+
+divide_yards = functools.partial(bring_kinds, which_dim=0)
 
 
 def body(dec_inputs, w_query, w_key, w_value, ctx_grad, encoded, enc_lengths):
@@ -19,10 +38,7 @@
     query = jnp.dot(inputs, wq_own, preferred_element_type=jnp.float32).astype(jnp.bfloat16)
     key = jnp.dot(encoded, wk_own, preferred_element_type=jnp.float32).astype(jnp.bfloat16)
     value = jnp.dot(encoded, wv_own, preferred_element_type=jnp.float32).astype(jnp.bfloat16)
-    key_all, value_all = (
-        lax.all_gather(key, "seq", axis=0, tiled=True),
-        lax.all_gather(value, "seq", axis=0, tiled=True),
-    )
+    key_all, value_all = (divide_yards(key), lax.all_gather(value, "seq", axis=0, tiled=True))
     limit = jnp.broadcast_to(enc_lengths[:, None], (blocks, kdev)).reshape(-1)
     slots = lax.broadcasted_iota(jnp.int32, (blocks, kdev), 1).reshape(-1)
     valid = (slots < limit)[None, :]

time: 164 us -> 157 us (0.957)
  blocking collectives: 29.8 us -> 15.1 us
  starting transfers between devices: 0.16 us -> 6.66 us
    all_gather x1 -> x0, blocking collectives: 15.6 us -> none  [body(): lax.all_gather(key, 'seq', axis=0, tiled=True)]
    ppermute x0 -> x2, starting transfers between devices: none -> 6.5 us  [bring_kinds(): lax.ppermute(step_out, 'seq', [(tick, (tick - plain) % value_now) for tic...]
  transfers between devices with their start and end apart: 4 -> 6, of which waited for: 4 -> 5; matrix products, arithmetic and copies ran while one was open for 4% -> 5% of each run, Pallas kernels for 0% -> 0%
where the time goes in v1:
time: 157 us
  waiting for transfers between devices  103 us (66%)
  matrix products  16.9 us (11%)
  blocking collectives  15.1 us (10%)
  between operations  13.9 us (9%)
  starting transfers between devices  6.66 us (4%)
    reduce_scatter x1, waiting for transfers between devices, body(): lax.psum_scatter(input_term.astype(jnp.bfloat16), 'tensor', scatter_dimen...  34.5 us
    reduce_scatter x1, waiting for transfers between devices, body(): lax.psum_scatter(encoder_term.astype(jnp.bfloat16), ('tensor', 'section')...  31.4 us
    reduce_scatter x1, waiting for transfers between devices, body(): lax.psum_scatter(dkey_part.astype(jnp.bfloat16), 'seq', scatter_dimension...  19.7 us
    reduce_scatter x1, waiting for transfers between devices, body(): lax.psum_scatter(dvalue_part.astype(jnp.bfloat16), 'seq', scatter_dimensi...  16.5 us
    all_gather x1, blocking collectives, body(): lax.all_gather(value, 'seq', axis=0, tiled=True)  15.1 us
    ppermute x2, starting transfers between devices, bring_kinds(): lax.ppermute(step_out, 'seq', [(tick, (tick - plain) % value_now) for tic...  6.5 us
    dot_general x1, matrix products, body(): jnp.einsum('kd,ed->ke', dvalue, wv_own, preferred_element_type=jnp.float32)  3.86 us
    dot_general x1, matrix products, body(): jnp.einsum('kd,ed->ke', dkey, wk_own, preferred_element_type=jnp.float32)  3.66 us
  transfers between devices with their start and end apart: 6, of which 5 were waited for; matrix products, arithmetic and copies ran while one was open for 5% of the time, Pallas kernels for 0%

profile of v1, /device:TPU:0, one launch (start us, length us, event | category | flops | bytes accessed | tf_op | source)
XLA Modules:
  0.0 156.6 jit_solution(4859808542436453612)
XLA Ops:
  7.2 0.0 copy-start
  7.2 0.0 copy-start.2
  7.2 0.0 reduce-scatter.7.cloned.1.call-start
  7.2 0.0 copy-start.1
  7.2 2.5 %constant_dynamic-update-slice_fusion.5 = (bf16[896,256]{1,0:T(8,128)(2,1)S(1)}, bf16[112,256]{1,0:T(8,128)(2,1)S(1)}) fusion(bf16[112,4096]{1,0:T(8,128)(2,1)} %param.12, bf16[1,4096,256]{2,1,0:T(8,128)(2,1)} %param.9), kind=kOutput, calls=%fused_computation.39 | convolution fusion | flops 234909696 | bytes 3129344 | tf_op jit(solution)/shard_map/dot_general | solution.py:39
  9.7 0.0 copy-start.3
  9.7 0.0 copy-start.4
  9.7 5.1 %collective-permute-start = (bf16[112,256]{1,0:T(8,128)(2,1)S(1)}, bf16[112,256]{1,0:T(8,128)(2,1)S(1)}, u32[]{:S(2)}, u32[]{:S(2)}) collective-permute-start(bf16[112,256]{1,0:T(8,128)(2,1)S(1)} %get-tuple-element.3), channel_id=1, source_target_pairs={{0,24},{8,0},{16,8},{24,16},{1,25},{9,1},{17,9},{25,17},{2,26},{10... | collective-permute-start | bytes 172040 | tf_op jit(solution)/shard_map/ppermute | solution.py:17
  14.8 0.0 copy-done.2
  14.8 0.0 copy-done.1
  14.8 0.5 fusion.21
  15.4 0.0 copy-done
  15.4 0.0 copy-done.4
  15.4 0.0 copy-start.6
  15.4 0.7 fusion.13
  16.1 0.0 copy-done.6
  16.1 0.0 copy-start.5
  16.1 0.1 iota_compare_fusion
  16.2 0.5 collective-permute-done
  16.7 0.0 copy-done.3
  16.7 1.4 collective-permute-start.1
  18.1 15.1 %all_gather.3 = bf16[448,256]{1,0:T(8,128)(2,1)} all-gather(bf16[112,256]{1,0:T(8,128)(2,1)S(1)} %fusion.21), channel_id=1, replica_groups=mesh['seq'=4,'tensor'=2,'section'=4] {'seq'}, dimensions={0}, use_global_device_ids=true | all-gather | bytes 286720 | tf_op jit(solution)/shard_map/all_gather | solution.py:41
  33.2 0.1 lt.23
  33.3 0.0 collective-permute-done.1
  33.3 0.8 constant_dynamic-update-slice_fusion.2
  34.1 0.3 fusion.36
  34.4 0.1 fusion.25
  34.6 0.0 copy-done.5
  34.6 1.2 multiply_reduce_fusion
  35.8 0.2 multiply_convert_fusion
  36.0 0.9 convolution_convert_fusion.2
  36.9 0.0 reduce-scatter.7.cloned.1.call-update
  36.9 0.0 reduce-scatter.9.cloned.1.call-start
  37.0 1.0 convolution_convert_fusion.1
  38.0 0.0 reduce-scatter.9.cloned.1.call-update
  38.0 0.0 reduce-scatter.11.cloned.1.call-start
  38.0 19.7 %reduce-scatter.7.cloned.1.call-done = bf16[112,256]{1,0:T(8,128)(2,1)} async-done(((bf16[448,256]{1,0:T(8,128)(2,1)}), bf16[112,256]{1,0:T(8,128)(2,1)}) %reduce-scatter.7.cloned.1.call-update) | async-done | bytes 57360 | tf_op jit(solution)/shard_map/reduce_scatter | solution.py:58
  57.7 3.7 %fusion.4 = f32[112,4096]{1,0:T(8,128)} fusion(bf16[112,256]{1,0:T(8,128)(2,1)} %reduce-scatter.7.cloned.1.call-done, bf16[1,4096,256]{2,1,0:T(8,128)(2,1)} %param.9), kind=kOutput, calls=%fused_computation.6 | convolution fusion | flops 234881024 | bytes 3989504 | tf_op jit(solution)/shard_map/kd,ed->ke/dot_general | solution.py:71
  61.3 16.5 %reduce-scatter.9.cloned.1.call-done = bf16[112,256]{1,0:T(8,128)(2,1)} async-done(((bf16[448,256]{1,0:T(8,128)(2,1)}), bf16[112,256]{1,0:T(8,128)(2,1)}) %reduce-scatter.9.cloned.1.call-update) | async-done | bytes 57360 | tf_op jit(solution)/shard_map/reduce_scatter | solution.py:61
  77.8 3.9 %fusion = bf16[112,4096]{1,0:T(8,128)(2,1)} fusion(f32[112,4096]{1,0:T(8,128)} %fusion.4, bf16[112,256]{1,0:T(8,128)(2,1)} %reduce-scatter.9.cloned.1.call-done, bf16[1,4096,256]{2,1,0:T(8,128)(2,1)} %param.10), kind=kOutput, calls=%fused_computation.2 | convolution fusion | flops 235798528 | bytes 4907008 | tf_op jit(solution)/shard_map/kd,ed->ke/dot_general | solution.py:72
  81.7 0.0 reduce-scatter.11.cloned.1.call-update
  81.7 0.0 reduce-scatter.5.cloned.1.call-start
  81.8 2.3 %convolution_convert_fusion = bf16[256,4096]{1,0:T(8,128)(2,1)} fusion(bf16[1,4096,256]{2,1,0:T(8,128)(2,1)S(1)} %copy-done, bf16[256,448]{0,1:T(8,128)(2,1)S(1)} %multiply_convert_fusion, bf16[896,256]{1,0:T(8,128)(2,1)S(1)} %constant_dynamic-update-slice_fusion, s32[]{:T(128)S(6)} %select_n.21), kind=kOutput, calls=%fused_computation | convolution fusion | flops 596705280 | bytes 4653060 | tf_op jit(solution)/shard_map/qd,ed->qe/dot_general | solution.py:67
  84.1 0.0 reduce-scatter.5.cloned.1.call-update
  84.1 31.4 %reduce-scatter.11.cloned.1.call-done = bf16[112,512]{1,0:T(8,128)(2,1)} async-done(((bf16[112,4096]{1,0:T(8,128)(2,1)}), bf16[112,512]{1,0:T(8,128)(2,1)}) %reduce-scatter.11.cloned.1.call-update) | async-done | bytes 114704 | tf_op jit(solution)/shard_map/reduce_scatter | solution.py:75
  115.5 34.5 %reduce-scatter.5.cloned.1.call-done = bf16[256,2048]{1,0:T(8,128)(2,1)} async-done(((bf16[256,4096]{1,0:T(8,128)(2,1)}), bf16[256,2048]{1,0:T(8,128)(2,1)}) %reduce-scatter.5.cloned.1.call-update) | async-done | bytes 1048592 | tf_op jit(solution)/shard_map/reduce_scatter | solution.py:68
  (5 shorter events, 0.0 us)
Async XLA Ops:
  7.2 8.2 %copy-start = (bf16[1,4096,256]{2,1,0:T(8,128)(2,1)S(1)}, bf16[1,4096,256]{2,1,0:T(8,128)(2,1)}, u32[]{:S(2)}) copy-start(bf16[1,4096,256]{2,1,0:T(8,128)(2,1)} %param.8) | copy-start | bytes 6291460
  7.2 7.7 %copy-start.2 = (bf16[112,4096]{1,0:T(8,128)(2,1)S(1)}, bf16[112,4096]{1,0:T(8,128)(2,1)}, u32[]{:S(2)}) copy-start(bf16[112,4096]{1,0:T(8,128)(2,1)} %param.12) | copy-start | bytes 2752516
  7.2 50.5 %reduce-scatter.7.cloned.1.call-start = ((), (), s32[]{:S(2)}) async-start(), calls=%async_computation.5 | async-start | bytes 286720 | tf_op jit(solution)/shard_map/reduce_scatter | solution.py:58
  7.2 7.6 %copy-start.1 = (bf16[1,4096,256]{2,1,0:T(8,128)(2,1)S(1)}, bf16[1,4096,256]{2,1,0:T(8,128)(2,1)}, u32[]{:S(2)}) copy-start(bf16[1,4096,256]{2,1,0:T(8,128)(2,1)} %param.10) | copy-start | bytes 6291460
  9.7 7.0 %copy-start.3 = (bf16[112,256]{1,0:T(8,128)(2,1)}, bf16[112,256]{1,0:T(8,128)(2,1)S(1)}, u32[]{:S(2)}) copy-start(bf16[112,256]{1,0:T(8,128)(2,1)S(1)} %get-tuple-element.3) | copy-start | bytes 172036
  9.7 5.6 %copy-start.4 = (bf16[1,256,4096]{2,1,0:T(8,128)(2,1)S(1)}, bf16[1,256,4096]{2,1,0:T(8,128)(2,1)}, u32[]{:S(2)}) copy-start(bf16[1,256,4096]{2,1,0:T(8,128)(2,1)} %param.7) | copy-start | bytes 6291460
  9.7 6.9 %collective-permute-start = (bf16[112,256]{1,0:T(8,128)(2,1)S(1)}, bf16[112,256]{1,0:T(8,128)(2,1)S(1)}, u32[]{:S(2)}, u32[]{:S(2)}) collective-permute-start(bf16[112,256]{1,0:T(8,128)(2,1)S(1)} %get-tuple-element.3), channel_id=1, source_target_pairs={{0,24},{8,0},{16,8},{24,16},{1,25},{9,1},{17,9},{25,17},{2,26},{10... | collective-permute-start | bytes 172040 | tf_op jit(solution)/shard_map/ppermute | solution.py:17
  15.4 0.7 copy-start.6
  16.1 18.5 %copy-start.5 = (bf16[1,256,256]{2,1,0:T(8,128)(2,1)S(1)}, bf16[1,256,256]{2,1,0:T(8,128)(2,1)}, u32[]{:S(2)}) copy-start(bf16[1,256,256]{2,1,0:T(8,128)(2,1)} %param.11) | copy-start | bytes 393220
  16.7 16.6 %collective-permute-start.1 = (bf16[224,256]{1,0:T(8,128)(2,1)S(1)}, bf16[224,256]{1,0:T(8,128)(2,1)S(1)}, u32[]{:S(2)}, u32[]{:S(2)}) collective-permute-start(bf16[224,256]{1,0:T(8,128)(2,1)S(1)} %pad_maximum_fusion), channel_id=1, source_target_pairs={{0,16},{8,24},{16,0},{24,8},{1,17},{9,25},{17,1},{25,9},{2,18},{10... | collective-permute-start | bytes 344072 | tf_op jit(solution)/shard_map/ppermute | solution.py:17
  36.9 40.9 %reduce-scatter.9.cloned.1.call-start = ((), (), s32[]{:S(2)}) async-start(), calls=%async_computation.6 | async-start | bytes 286720 | tf_op jit(solution)/shard_map/reduce_scatter | solution.py:61
  38.0 77.6 %reduce-scatter.11.cloned.1.call-start = ((), (), s32[]{:S(2)}) async-start(), calls=%async_computation.7 | async-start | bytes 1032192 | tf_op jit(solution)/shard_map/reduce_scatter | solution.py:75
  81.7 68.4 %reduce-scatter.5.cloned.1.call-start = ((), (), s32[]{:S(2)}) async-start(), calls=%async_computation.4 | async-start | bytes 3145728 | tf_op jit(solution)/shard_map/reduce_scatter | solution.py:68
Sparse Core Ops, SparseCore 0:
  37.1 20.5 reduce-scatter.6
  60.0 17.7 reduce-scatter.8
  81.8 33.6 reduce-scatter.10
  118.2 31.8 reduce-scatter.4
